TPU v7x, 32 devices: a whole 2x2x4 slice. The times are simulated.
32 devices in a mesh: fsdp: 16 (over z, y, core), dp: 2 (over x).
Axes of the slice: x: 2, y: 2, z: 4, core: 2. Of those that a mesh axis runs over, the one named last changes fastest.
Arguments:
- tokens: bfloat16 [32, 256, 1152], P(('fsdp', 'dp')), may hold values from -12 to 12, as said below
- cond: bfloat16 [32, 1152], P(('fsdp', 'dp')), may hold values from -6 to 6
- segment_ids: int32 [32, 256], P(('fsdp', 'dp')), may hold values from 0 to 7, as said below
- ada_weight: bfloat16 [1152, 6912], P('fsdp'), may hold values from -0.1875 to 0.1875
- ada_bias: bfloat16 [6912], P('fsdp'), may hold values from -1 to 1
- qkv_weight: bfloat16 [1152, 3456], P('fsdp'), may hold values from -0.1875 to 0.1875
- qv_bias: bfloat16 [2304], P('fsdp'), may hold values from -1 to 1
- proj_weight: bfloat16 [1152, 1152], P('fsdp'), may hold values from -0.75 to 0.75
- proj_bias: bfloat16 [1152], P('fsdp'), may hold values from -1 to 1
- fc1_weight: bfloat16 [1152, 4608], P('fsdp'), may hold values from -0.1875 to 0.1875
- fc1_bias: bfloat16 [4608], P('fsdp'), may hold values from -1 to 1
- fc2_weight: bfloat16 [4608, 1152], P('fsdp'), may hold values from -0.09375 to 0.09375
- fc2_bias: bfloat16 [1152], P('fsdp'), may hold values from -1 to 1
- out_grad: bfloat16 [32, 256, 1152], P(('fsdp', 'dp')), may hold values from -6 to 6
Outputs:
- output: bfloat16 [32, 256, 1152], P(('fsdp', 'dp'))
- tokens_grad: bfloat16 [32, 256, 1152], P(('fsdp', 'dp'))
- ada_weight_grad: float32 [1152, 6912], P('fsdp')
- ada_bias_grad: float32 [6912], P('fsdp')
- qkv_weight_grad: float32 [1152, 3456], P('fsdp')
- qv_bias_grad: float32 [2304], P('fsdp')
- proj_weight_grad: float32 [1152, 1152], P('fsdp')
- proj_bias_grad: float32 [1152], P('fsdp')
- fc1_weight_grad: float32 [1152, 4608], P('fsdp')
- fc1_bias_grad: float32 [4608], P('fsdp')
- fc2_weight_grad: float32 [4608, 1152], P('fsdp')
- fc2_bias_grad: float32 [1152], P('fsdp')
Inputs may be any that keep to these rules, and one draw needn't show every extreme that they name: `segment_ids`: each row holds whole images one after another, numbered from 0 in order: eight images of 32 tokens, or two of 128 tokens, or one of 128 tokens among four of 32 tokens. Some row holds eight images and some row holds two. `tokens`: token features.
All inputs are finite; a program needn't handle non-finite values.
Results may differ from a plain program's by a relative error of at most 0.02.
The roundings to bfloat16 on the way count: a program that leaves them out, or rounds other values in their place, can miss the bound.
Values may be sent and summed in bfloat16 or wider, within the bound.
A program may use at most 384 MiB of HBM per device.

v0:
```python
import functools

import jax
import jax.numpy as jnp
from jax import lax
from jax.experimental import pallas as pl
from jax.experimental.pallas import tpu as pltpu
from jax.sharding import PartitionSpec as P

HEADS = 16
HEAD_DIM = 72


root_half = 0.7978845608028654
norm_eps = 1e-06
masked_score = -1e30


def gelu_tanh(stream):
    return (
        0.5 * stream * (1.0 + jnp.tanh(root_half * (stream + 0.044715 * stream * stream * stream)))
    )


def gelu_slope(stream):
    tanh_inner = jnp.tanh(root_half * (stream + 0.044715 * stream * stream * stream))
    return 0.5 * (1.0 + tanh_inner) + 0.5 * stream * (1.0 - tanh_inner * tanh_inner) * root_half * (
        1.0 + 3.0 * 0.044715 * stream * stream
    )


def normalize(stream):
    centre = jnp.mean(stream, axis=-1, keepdims=True)
    centred = stream - centre
    inv_std = lax.rsqrt(jnp.mean(centred * centred, axis=-1, keepdims=True) + norm_eps)
    return (centred * inv_std, inv_std)


def normalize_back(incoming, normed, inv_std):
    return inv_std * (
        incoming
        - jnp.mean(incoming, axis=-1, keepdims=True)
        - normed * jnp.mean(incoming * normed, axis=-1, keepdims=True)
    )


def head_scores(projected, same_doc, head_index, model_width):
    query_part = lax.dynamic_slice_in_dim(projected, head_index * HEAD_DIM, HEAD_DIM, 1)
    key_part = lax.dynamic_slice_in_dim(projected, model_width + head_index * HEAD_DIM, HEAD_DIM, 1)
    value_part = lax.dynamic_slice_in_dim(
        projected, 2 * model_width + head_index * HEAD_DIM, HEAD_DIM, 1
    )
    raw_scores = jnp.einsum(
        "qd,kd->qk", query_part, key_part, preferred_element_type=jnp.float32
    ) * HEAD_DIM ** (-0.5)
    return (jnp.where(same_doc, raw_scores, masked_score), query_part, key_part, value_part)


def merge_heads(stacked, model_width):
    return jnp.transpose(stacked, (1, 0, 2)).reshape(stacked.shape[1], model_width)


def attend_row(projected, segments_row, model_width):
    same_doc = segments_row[:, None] == segments_row[None, :]

    def one_head(head_index):
        scores, query_part, key_part, value_part = head_scores(
            projected, same_doc, head_index, model_width
        )
        top_score = jnp.max(scores, axis=-1, keepdims=True)
        exp_scores = jnp.exp(scores - top_score)
        denominator = jnp.sum(exp_scores, axis=-1, keepdims=True)
        probabilities = (exp_scores / denominator).astype(jnp.bfloat16)
        mixed_heads = jnp.dot(probabilities, value_part, preferred_element_type=jnp.float32)
        return (mixed_heads, (top_score + jnp.log(denominator))[:, 0])

    mixed_heads, log_total = lax.map(one_head, jnp.arange(HEADS))
    return (merge_heads(mixed_heads, model_width).astype(jnp.bfloat16), log_total)


def attend_back(projected, segments_row, log_total, d_mixed, model_width):
    same_doc = segments_row[:, None] == segments_row[None, :]
    head_scale = HEAD_DIM ** (-0.5)

    def one_head(head_index):
        scores, query_part, key_part, value_part = head_scores(
            projected, same_doc, head_index, model_width
        )
        d_head = lax.dynamic_slice_in_dim(d_mixed, head_index * HEAD_DIM, HEAD_DIM, 1)
        lse_row = lax.dynamic_index_in_dim(log_total, head_index, 0, keepdims=False)
        probabilities = jnp.exp(scores - lse_row[:, None])
        prob_low = probabilities.astype(jnp.bfloat16)
        d_probs = jnp.einsum("qd,kd->qk", d_head, value_part, preferred_element_type=jnp.float32)
        d_value = jnp.einsum("qk,qd->kd", prob_low, d_head, preferred_element_type=jnp.float32)
        d_scores = (
            probabilities * (d_probs - jnp.sum(d_probs * probabilities, axis=-1, keepdims=True))
        ).astype(jnp.bfloat16)
        d_query = (
            jnp.einsum("qk,kd->qd", d_scores, key_part, preferred_element_type=jnp.float32)
            * head_scale
        )
        d_key = (
            jnp.einsum("qk,qd->kd", d_scores, query_part, preferred_element_type=jnp.float32)
            * head_scale
        )
        return (d_query, d_key, d_value)

    d_query, d_key, d_value = lax.map(one_head, jnp.arange(HEADS))
    merged = [
        merge_heads(d_query, model_width),
        merge_heads(d_key, model_width),
        merge_heads(d_value, model_width),
    ]
    return jnp.concatenate(merged, axis=-1).astype(jnp.bfloat16)


def general_form(
    tokens,
    cond,
    segment_ids,
    ada_weight,
    ada_bias,
    qkv_weight,
    qv_bias,
    proj_weight,
    proj_bias,
    fc1_weight,
    fc1_bias,
    fc2_weight,
    fc2_bias,
    out_grad,
):
    row_count, seq_len, model_width = tokens.shape
    ff_width = fc1_weight.shape[1]
    stream = tokens.astype(jnp.float32)
    cond_float = cond.astype(jnp.float32)
    cond_act = (cond_float / (1.0 + jnp.exp(-cond_float))).astype(jnp.bfloat16)
    fsdp_at, dp_at = lax.axis_index("fsdp"), lax.axis_index("dp")
    dp_size = lax.axis_size("dp")
    slice_width, bias_width = ada_weight.shape[0], ada_bias.shape[0]
    act_all = lax.all_gather(cond_act, ("fsdp", "dp"), axis=0, tiled=True)
    act_mine = lax.dynamic_slice_in_dim(act_all, fsdp_at * slice_width, slice_width, 1)
    partial = jnp.dot(act_mine, ada_weight, preferred_element_type=jnp.float32)
    bias_row = lax.dynamic_update_slice_in_dim(
        jnp.zeros((6 * model_width,), jnp.float32),
        ada_bias.astype(jnp.float32),
        fsdp_at * bias_width,
        0,
    )
    partial = (partial + bias_row).reshape(-1, dp_size, row_count, 6 * model_width)
    partial = lax.dynamic_index_in_dim(partial, dp_at, 1, keepdims=False)
    modulation = lax.psum_scatter(
        partial.reshape(-1, 6 * model_width), "fsdp", scatter_dimension=0, tiled=True
    )
    pieces = [
        modulation[:, None, section * model_width : (section + 1) * model_width]
        for section in range(6)
    ]
    shift_one, scale_one, gate_one, shift_two, scale_two, gate_two = pieces
    qkv_full, qv_bias_full, proj_full, proj_bias_full = (
        lax.all_gather(qkv_weight, "fsdp", axis=0, tiled=True),
        lax.all_gather(qv_bias, "fsdp", axis=0, tiled=True),
        lax.all_gather(proj_weight, "fsdp", axis=0, tiled=True),
        lax.all_gather(proj_bias, "fsdp", axis=0, tiled=True),
    )
    normed_one, inv_one = normalize(stream)
    hidden_one = (normed_one * (1.0 + scale_one) + shift_one).astype(jnp.bfloat16)
    qv_float = qv_bias_full.astype(jnp.float32)
    qkv_bias = jnp.concatenate(
        [qv_float[:model_width], jnp.zeros((model_width,), jnp.float32), qv_float[model_width:]]
    )
    projected = (
        jnp.dot(hidden_one, qkv_full, preferred_element_type=jnp.float32) + qkv_bias
    ).astype(jnp.bfloat16)

    def row_forward(row_items):
        return attend_row(row_items[0], row_items[1], model_width)

    mixed_rows, log_total = lax.map(row_forward, (projected, segment_ids))
    branch_one = jnp.dot(
        mixed_rows, proj_full, preferred_element_type=jnp.float32
    ) + proj_bias_full.astype(jnp.float32)
    resid_one = stream + gate_one * branch_one
    fc1_full, fc1_bias_full, fc2_full, fc2_bias_full = (
        lax.all_gather(fc1_weight, "fsdp", axis=0, tiled=True),
        lax.all_gather(fc1_bias, "fsdp", axis=0, tiled=True),
        lax.all_gather(fc2_weight, "fsdp", axis=0, tiled=True),
        lax.all_gather(fc2_bias, "fsdp", axis=0, tiled=True),
    )
    normed_two, inv_two = normalize(resid_one)
    hidden_two = (normed_two * (1.0 + scale_two) + shift_two).astype(jnp.bfloat16)
    pre_act = jnp.dot(
        hidden_two, fc1_full, preferred_element_type=jnp.float32
    ) + fc1_bias_full.astype(jnp.float32)
    active = gelu_tanh(pre_act).astype(jnp.bfloat16)
    branch_two = jnp.dot(
        active, fc2_full, preferred_element_type=jnp.float32
    ) + fc2_bias_full.astype(jnp.float32)
    output = (resid_one + gate_two * branch_two).astype(jnp.bfloat16)
    d_out = out_grad.astype(jnp.float32)
    fc1_back, fc2_back = (
        lax.all_gather(fc1_weight, "fsdp", axis=0, tiled=True),
        lax.all_gather(fc2_weight, "fsdp", axis=0, tiled=True),
    )
    d_gate_two = jnp.sum(d_out * branch_two, axis=1)
    d_branch_two = (d_out * gate_two).astype(jnp.bfloat16)
    fc2_shard = lax.psum_scatter(
        jnp.einsum("rsf,rsd->fd", active, d_branch_two, preferred_element_type=jnp.float32).astype(
            jnp.bfloat16
        ),
        "fsdp",
        scatter_dimension=0,
        tiled=True,
    )
    grad_fc2_bias = jnp.sum(d_branch_two.astype(jnp.float32), axis=(0, 1))
    d_active = jnp.einsum("rsd,fd->rsf", d_branch_two, fc2_back, preferred_element_type=jnp.float32)
    d_pre = (d_active * gelu_slope(pre_act)).astype(jnp.bfloat16)
    grad_fc1_bias = jnp.sum(d_pre.astype(jnp.float32), axis=(0, 1))
    d_hidden_two = jnp.einsum("rsf,ef->rse", d_pre, fc1_back, preferred_element_type=jnp.float32)
    d_scale_two = jnp.sum(d_hidden_two * normed_two, axis=1)
    d_shift_two = jnp.sum(d_hidden_two, axis=1)
    d_resid = d_out + normalize_back(d_hidden_two * (1.0 + scale_two), normed_two, inv_two)
    qkv_back, proj_back = (
        lax.all_gather(qkv_weight, "fsdp", axis=0, tiled=True),
        lax.all_gather(proj_weight, "fsdp", axis=0, tiled=True),
    )
    d_gate_one = jnp.sum(d_resid * branch_one, axis=1)
    d_branch_one = (d_resid * gate_one).astype(jnp.bfloat16)
    grad_proj_bias = jnp.sum(d_branch_one.astype(jnp.float32), axis=(0, 1))
    d_mixed = jnp.einsum(
        "rsd,ed->rse", d_branch_one, proj_back, preferred_element_type=jnp.float32
    ).astype(jnp.bfloat16)

    def row_backward(row_items):
        return attend_back(row_items[0], row_items[1], row_items[2], row_items[3], model_width)

    d_projected = lax.map(row_backward, (projected, segment_ids, log_total, d_mixed))
    d_proj_float = d_projected.astype(jnp.float32)
    grad_qv_bias = jnp.concatenate(
        [
            jnp.sum(d_proj_float[..., :model_width], axis=(0, 1)),
            jnp.sum(d_proj_float[..., 2 * model_width :], axis=(0, 1)),
        ]
    )
    d_hidden_one = jnp.einsum(
        "rsf,ef->rse", d_projected, qkv_back, preferred_element_type=jnp.float32
    )
    d_scale_one = jnp.sum(d_hidden_one * normed_one, axis=1)
    d_shift_one = jnp.sum(d_hidden_one, axis=1)
    tokens_grad = (
        d_resid + normalize_back(d_hidden_one * (1.0 + scale_one), normed_one, inv_one)
    ).astype(jnp.bfloat16)
    d_modulation = jnp.concatenate(
        [d_shift_one, d_scale_one, d_gate_one, d_shift_two, d_scale_two, d_gate_two], axis=-1
    ).astype(jnp.bfloat16)
    d_mod_all = lax.all_gather(d_modulation, ("fsdp", "dp"), axis=0, tiled=True)
    grad_ada = jnp.einsum("rd,re->de", act_mine, d_mod_all, preferred_element_type=jnp.float32)
    grad_ada_bias = jnp.sum(
        lax.dynamic_slice_in_dim(d_mod_all, fsdp_at * bias_width, bias_width, 1).astype(jnp.float32),
        axis=0,
    )

    def owners(term):
        return lax.psum_scatter(
            term.astype(jnp.bfloat16), "fsdp", scatter_dimension=0, tiled=True
        )

    qkv_shard = owners(
        jnp.einsum("rse,rsf->ef", hidden_one, d_projected, preferred_element_type=jnp.float32)
    )
    proj_shard = owners(
        jnp.einsum("rse,rsd->ed", mixed_rows, d_branch_one, preferred_element_type=jnp.float32)
    )
    fc1_shard = owners(
        jnp.einsum("rse,rsf->ef", hidden_two, d_pre, preferred_element_type=jnp.float32)
    )
    bias_shards = (
        None,
        lax.psum_scatter(
            grad_qv_bias.astype(jnp.bfloat16), "fsdp", scatter_dimension=0, tiled=True
        ).astype(jnp.float32),
        lax.psum_scatter(
            grad_proj_bias.astype(jnp.bfloat16), "fsdp", scatter_dimension=0, tiled=True
        ).astype(jnp.float32),
        lax.psum_scatter(
            grad_fc1_bias.astype(jnp.bfloat16), "fsdp", scatter_dimension=0, tiled=True
        ).astype(jnp.float32),
        lax.psum_scatter(
            grad_fc2_bias.astype(jnp.bfloat16), "fsdp", scatter_dimension=0, tiled=True
        ).astype(jnp.float32),
    )
    summed = (
        grad_ada,
        grad_ada_bias,
        lax.psum(qkv_shard.astype(jnp.bfloat16), "dp").astype(jnp.float32),
        lax.psum(bias_shards[1].astype(jnp.bfloat16), "dp").astype(jnp.float32),
        lax.psum(proj_shard.astype(jnp.bfloat16), "dp").astype(jnp.float32),
        lax.psum(bias_shards[2].astype(jnp.bfloat16), "dp").astype(jnp.float32),
        lax.psum(fc1_shard.astype(jnp.bfloat16), "dp").astype(jnp.float32),
        lax.psum(bias_shards[3].astype(jnp.bfloat16), "dp").astype(jnp.float32),
        lax.psum(fc2_shard, "dp").astype(jnp.float32),
        lax.psum(bias_shards[4].astype(jnp.bfloat16), "dp").astype(jnp.float32),
    )
    return (
        output,
        tokens_grad,
        summed[0],
        summed[1],
        summed[2],
        summed[3],
        summed[4],
        summed[5],
        summed[6],
        summed[7],
        summed[8],
        summed[9],
    )


MESH_ID = pl.DeviceIdType.MESH
f32 = jnp.float32
bf16 = jnp.bfloat16

SEQ = 256
WIDTH = 1152
HIDDEN = 4608
PART = 1152
QKV = 864
PAD = 128
LOCAL = 4


def dot_nn(left, right):
    return lax.dot_general(left, right, (((1,), (0,)), ((), ())), preferred_element_type=f32)


def dot_nt(left, right):
    return lax.dot_general(left, right, (((1,), (1,)), ((), ())), preferred_element_type=f32)


def dot_tn(left, right):
    return lax.dot_general(left, right, (((0,), (0,)), ((), ())), preferred_element_type=f32)


def iota(shape, axis):
    return lax.broadcasted_iota(jnp.int32, shape, axis)


def whole_part(value, divisor):
    return jnp.floor((value + 0.5) * (1.0 / divisor))


class Ids:
    def __init__(self):
        self.used = 0

    def take(self, count):
        start = self.used
        self.used += count
        return start


IDS = Ids()
IDS.small_y, IDS.small_z, IDS.small_c = IDS.take(1), IDS.take(6), IDS.take(1)
IDS.small_x, IDS.small_d = IDS.take(1), IDS.take(1)
IDS.mod_c, IDS.mod_y, IDS.mod_z = IDS.take(1), IDS.take(1), IDS.take(3)
IDS.core = [IDS.take(1) for _ in range(3)]
IDS.z = [IDS.take(3) for _ in range(4)]
IDS.y = [IDS.take(4) for _ in range(4)]
IDS.h1, IDS.h2, IDS.d2, IDS.d1 = IDS.take(3), IDS.take(3), IDS.take(3), IDS.take(3)
IDS.r1, IDS.r2, IDS.r3, IDS.r4 = IDS.take(3), IDS.take(3), IDS.take(3), IDS.take(3)
IDS.gy = [IDS.take(4) for _ in range(4)]
IDS.gz = [IDS.take(3) for _ in range(4)]
IDS.gf = [IDS.take(3) for _ in range(4)]
IDS.end_y, IDS.end_z, IDS.end_x, IDS.end_c = IDS.take(1), IDS.take(6), IDS.take(1), IDS.take(1)
ID_COUNT = IDS.used

SCRATCH = (
    ((32, 8, 384), f32),
    ((16, 8, WIDTH), f32),
    ((8, 8, WIDTH), f32),
    ((4, 8, WIDTH), f32),
    ((3, 8, WIDTH), f32),
    ((8, WIDTH), f32),
    ((72, WIDTH), bf16),
    ((72, QKV), bf16),
    ((72, PART), bf16),
    ((72, WIDTH), bf16),
    ((WIDTH, QKV), bf16),
    ((WIDTH, PART), bf16),
    ((PART, WIDTH), bf16),
    ((4, 72, WIDTH), bf16),
    ((288, WIDTH), bf16),
    ((1024, WIDTH), bf16),
    ((1024, WIDTH), bf16),
    ((1024, WIDTH), bf16),
    ((1024, 12 * PAD), bf16),
    ((16, SEQ, SEQ), bf16),
    ((1024, 288), bf16),
    ((1024, PART), bf16),
    ((1024, PART), bf16),
    ((1024, QKV), bf16),
    ((3, SEQ, WIDTH), bf16),
    ((3, SEQ, WIDTH), bf16),
    ((SEQ, WIDTH), bf16),
    ((SEQ, WIDTH), bf16),
    ((SEQ, WIDTH), bf16),
    ((SEQ, WIDTH), f32),
    ((SEQ, WIDTH), f32),
    ((SEQ, WIDTH), f32),
    ((SEQ, WIDTH), f32),
    ((16, WIDTH), f32),
    ((8, WIDTH), f32),
    ((WIDTH, QKV), bf16),
    ((WIDTH, PART), bf16),
    ((PART, WIDTH), bf16),
    ((4, 72, WIDTH), bf16),
    ((4, 144, QKV), bf16),
    ((4, 144, PART), bf16),
    ((4, 144, WIDTH), bf16),
    ((4, 72, WIDTH), bf16),
    ((3, 144, QKV), bf16),
    ((3, 144, PART), bf16),
    ((3, 144, WIDTH), bf16),
    ((3, 72, WIDTH), bf16),
    ((72, QKV), bf16),
    ((72, PART), bf16),
    ((72, WIDTH), bf16),
    ((72, QKV), bf16),
    ((72, PART), bf16),
    ((72, WIDTH), bf16),
    ((4, 72, QKV), bf16),
    ((4, 72, PART), bf16),
    ((4, 72, WIDTH), bf16),
    ((72, WIDTH), bf16),
    ((32, 16, WIDTH), bf16),
)


def block_kernel(
    tok, og, small, ada, adab, wqkv, wproj, wfc1, wfc2, out,
    tgrad, oada, oqkv, oproj, ofc1, ofc2, osum, S, modp, modc,
    mody, modz, mod, own_fc2, xr_qkv, xr_fc1, xr_fc2, G_qkv,
    G_fc1, G_fc2, G_proj, W_proj, H1, H2, D2, qp, P, mixed,
    active, slope, dprj, rrA, rrB, sA, sB, sX, keep, own,
    b1, resid, acc, bias, g_qkv, g_fc1, g_fc2, g_proj, yr_qkv, yr_fc1,
    yr_fc2, yr_proj, zr_qkv, zr_fc1, zr_fc2, zr_proj, fa_qkv, fa_fc1, fa_fc2, fb_qkv,
    fb_fc1, fb_fc2, fr_qkv, fr_fc1, fr_fc2, p_out, E, snd, rcv, loc,
):
    xr_w, G_w = (xr_qkv, xr_fc1, xr_fc2), (G_qkv, G_fc1, G_fc2)
    yr_w, zr_w = (yr_qkv, yr_fc1, yr_fc2), (zr_qkv, zr_fc1, zr_fc2)
    fa_w, fb_w, fr_w = (fa_qkv, fa_fc1, fa_fc2), (fb_qkv, fb_fc1, fb_fc2), (fr_qkv, fr_fc1, fr_fc2)
    f = lax.axis_index("fsdp")
    x = lax.axis_index("dp")
    z = lax.div(f, 4)
    y = lax.rem(lax.div(f, 2), 2)
    c = lax.rem(f, 2)
    q = 2 * x + c
    qp_, qx_, qd_ = 2 * x + 1 - c, 2 * (1 - x) + c, 2 * (1 - x) + 1 - c

    def dev(zz, yy, cc, xx):
        return ((zz * 2 + yy) * 2 + cc, xx)

    mate, xnb, diag, ynb = dev(z, y, 1 - c, x), dev(z, y, c, 1 - x), dev(z, y, 1 - c, 1 - x), dev(z, 1 - y, c, x)

    def z_to(k):
        return lax.rem(z + k, 4)

    def z_from(k):
        return lax.rem(z + 4 - k, 4)

    def znb(k):
        return dev(z_to(k), y, c, x)

    def rc(src, dst, ident, to):
        return pltpu.make_async_remote_copy(
            src_ref=src, dst_ref=dst, send_sem=snd.at[ident], recv_sem=rcv.at[ident],
            device_id=to, device_id_type=MESH_ID,
        )

    pending = []

    def send(src, dst, ident, to):
        rc(src, dst, ident, to).start()
        pending.append((src, ident, to))

    def got(dst, ident):
        rc(dst, dst, ident, mate).wait_recv()

    def sent(src, ident):
        rc(src, src, ident, mate).wait_send()

    def settle(first):
        keep_on = []
        for item in pending:
            if item[1] in first:
                sent(item[0], item[1])
            else:
                keep_on.append(item)
        pending[:] = keep_on

    barrier = pltpu.get_barrier_semaphore()
    neighbours = [mate, xnb, diag, ynb, znb(1), znb(2), znb(3)]
    for to in neighbours:
        pl.semaphore_signal(barrier, inc=1, device_id=to, device_id_type=MESH_ID)
    pl.semaphore_wait(barrier, len(neighbours))


    def slot_of(cc, xx, yy, zz):
        return ((cc * 2 + xx) * 2 + yy) * 4 + zz

    my_slot = slot_of(c, x, y, z)
    send(small, S.at[my_slot], IDS.small_y, ynb)
    own_copy = pltpu.make_async_copy(wfc2.at[q], own_fc2, loc.at[0])
    own_copy.start()
    send(wfc2.at[qp_], xr_fc2, IDS.core[2], mate)

    def split_qkv():
        for at in range(4):
            fr_qkv[at] = jnp.concatenate(
                [wqkv[:, (4 * step + at) * 72 : (4 * step + at + 1) * 72] for step in range(12)], axis=1
            )
        send(fr_qkv.at[qp_], xr_qkv, IDS.core[0], mate)

    def split_fc1():
        for at in range(4):
            fr_fc1[at] = jnp.concatenate(
                [wfc1[:, (4 * step + at) * 72 : (4 * step + at + 1) * 72] for step in range(16)], axis=1
            )
        send(fr_fc1.at[qp_], xr_fc1, IDS.core[1], mate)

    split_qkv()
    S[my_slot] = small[...]
    acc[...] = jnp.zeros((16, WIDTH), f32)
    in_column = y == x
    proj_copy = pltpu.make_async_copy(wproj, G_proj.at[z], loc.at[1])

    def chip_rows(zz, yy):
        return pl.ds(pl.multiple_of((2 * zz + yy) * 144, 16), 144)

    def own_part(kind):
        return G_w[kind].at[chip_rows(z, y), :]

    def assemble(kind):
        got(xr_w[kind], IDS.core[kind])
        mine = (own_fc2[...] if kind == 2 else fr_w[kind][q]).astype(f32)
        other = xr_w[kind][...].astype(f32)
        low = jnp.where(c == 0, mine, other)
        high = jnp.where(c == 0, other, mine)
        G_w[kind][chip_rows(z, y), :] = jnp.concatenate([low, high], axis=0).astype(bf16)

    def own_y(kind):
        send(own_part(kind), own_part(kind), IDS.y[kind], ynb)

    def own_z(kind, steps):
        for k in steps:
            send(own_part(kind), own_part(kind), IDS.z[kind] + k - 1, znb(k))

    STEPS = (1, 3, 2)

    def forward(kind, k):
        part = G_w[kind].at[chip_rows(z_from(k), y), :]
        got(part, IDS.z[kind] + k - 1)
        send(part, part, IDS.y[kind] + k, ynb)

    def arrived(kind):
        other = 1 - y
        got(G_w[kind].at[chip_rows(z, other), :], IDS.y[kind])
        for k in STEPS:
            got(G_w[kind].at[chip_rows(z_from(k), other), :], IDS.y[kind] + k)

    def proj_z():
        @pl.when(in_column)
        def _():
            proj_copy.start()
            for k in STEPS:
                rc(wproj, G_proj.at[z], IDS.z[3] + k - 1, znb(k)).start()

    def proj_y():
        @pl.when(in_column)
        def _():
            rc(wproj, G_proj.at[z], IDS.y[3], ynb).start()

    def proj_forward(k):
        @pl.when(in_column)
        def _():
            part = G_proj.at[z_from(k)]
            got(part, IDS.z[3] + k - 1)
            rc(part, part, IDS.y[3] + k, ynb).start()

    def proj_arrived():
        @pl.when(in_column)
        def _():
            proj_copy.wait()
            for k in (1, 2, 3):
                sent(wproj, IDS.z[3] + k - 1)
            sent(wproj, IDS.y[3])
            for k in STEPS:
                sent(G_proj.at[z_from(k)], IDS.y[3] + k)

        @pl.when(jnp.logical_not(in_column))
        def _():
            got(G_proj.at[z], IDS.y[3])
            for k in STEPS:
                got(G_proj.at[z_from(k)], IDS.y[3] + k)

        W_proj[...] = jnp.concatenate(
            [G_proj[head].astype(f32) for head in range(LOCAL)], axis=0
        ).astype(bf16)

    got(S.at[slot_of(c, x, 1 - y, z)], IDS.small_y)
    for k in (2, 1, 3):
        for yy in range(2):
            part = S.at[slot_of(c, x, yy, z)]
            send(part, part, IDS.small_z + 2 * (k - 1) + yy, znb(k))
    assemble(0)
    own_y(0)
    own_z(0, (1, 3))
    for k in (1, 2, 3):
        for yy in range(2):
            got(S.at[slot_of(c, x, yy, z_from(k))], IDS.small_z + 2 * (k - 1) + yy)
    eight = lambda cc, xx: S.at[pl.ds((cc * 2 + xx) * 8, 8)]
    send(eight(c, x), eight(c, x), IDS.small_c, mate)
    send(eight(c, x), eight(c, x), IDS.small_x, xnb)
    split_fc1()

    def pick_columns(rows):
        total = None
        for piece in range(3):
            kk = iota((384, PAD), 0) + piece * 384
            jj = iota((384, PAD), 1)
            chosen = ((kk == 72 * f + jj) & (jj < 72)).astype(f32).astype(bf16)
            term = dot_nn(rows(piece), chosen)
            total = term if total is None else total + term
        return total.astype(bf16)

    got(eight(1 - c, x), IDS.small_c)
    act = pick_columns(
        lambda piece: jnp.concatenate(
            [S[pl.ds((cc * 2 + x) * 8, 8), piece, :] for cc in range(2)], axis=0
        ).astype(bf16)
    )[:, :72]
    for section in range(6):
        modp[:, section, :] = dot_nn(
            act, ada[:, section * WIDTH : (section + 1) * WIDTH]
        ) + adab[section : section + 1, :]
    for section in (6, 7):
        modp[:, section, :] = jnp.zeros((16, WIDTH), f32)
    theirs, ours = modp.at[pl.ds((1 - c) * 8, 8)], modp.at[pl.ds(c * 8, 8)]
    send(theirs, modc, IDS.mod_c, mate)
    own_copy.wait()
    assemble(1)
    assemble(2)
    got(modc, IDS.mod_c)
    for at in range(8):
        ours[at] += modc[at]
    send(modp.at[pl.ds(c * 8 + (1 - y) * 4, 4)], mody, IDS.mod_y, ynb)
    forward(0, 1)
    got(mody, IDS.mod_y)
    base = c * 8 + y * 4
    for at in range(4):
        modp[base + at] += mody[at]
    for k in (2, 1, 3):
        send(modp.at[base + z_to(k)], modz.at[k - 1], IDS.mod_z + k - 1, znb(k))
    own_z(0, (2,))
    proj_z()
    own_z(1, STEPS)
    own_z(2, STEPS)
    proj_y()
    own_y(1)
    got(eight(c, 1 - x), IDS.small_x)
    send(eight(c, 1 - x), eight(c, 1 - x), IDS.small_d, mate)

    def place(row, width, lane_of, owner_of):
        kk = iota((384, width), 1).astype(f32)
        jj = iota((384, width), 0).astype(f32)
        chosen = (jj == lane_of(kk)).astype(f32).astype(bf16)
        spread = dot_nn(row.astype(bf16), chosen)
        at = iota((16, width), 0)
        slot_f = ((lax.rem(at, 4) * 2 + lax.rem(lax.div(at, 4), 2)) * 2 + lax.div(at, 8)).astype(f32)
        mine = slot_f == owner_of(iota((16, width), 1).astype(f32))
        return jnp.sum(jnp.where(mine, spread, 0.0), axis=0, keepdims=True)

    def plane(piece):
        return jnp.concatenate([S[pl.ds((cc * 2 + x) * 8, 8), piece, :] for cc in range(2)], axis=0)

    def mod72(kk):
        return kk - 72.0 * whole_part(kk, 72)

    by72 = lambda kk: whole_part(kk, 72)
    qf, xf, cf = q.astype(f32), x.astype(f32), c.astype(f32)
    row3, row4 = plane(3), plane(4)
    bias[0:1, :] = place(row3, WIDTH, lambda kk: 144.0 + mod72(kk), by72)
    bias[1:2, :] = place(row3, WIDTH, lambda kk: 216.0 + mod72(kk), by72)
    bias[2:3, :] = place(row4, WIDTH, lambda kk: 72.0 * qf + mod72(kk), by72)

    def qkv_owner(kk):
        third = whole_part(kk, 288)
        head = whole_part(kk - 288.0 * third, 72)
        owner = 2.0 * head + xf + 4.0 * third
        return jnp.where((third == 1.0) | (third > 2.5), -1.0, owner)

    bias[3:4, :] = place(row3, WIDTH, lambda kk: 72.0 * cf + mod72(kk), qkv_owner)

    for k in (1, 2, 3):
        got(modz.at[k - 1], IDS.mod_z + k - 1)
    mod[...] = modp[base + z] + modz[0] + modz[1] + modz[2]

    def row_of(section):
        return mod[section : section + 1, :]

    def slot_rows(slot):
        return pl.ds(pl.multiple_of(slot * SEQ, SEQ), SEQ)

    TILE = 64

    def tiles(body):
        def step(at, carry):
            body(pl.multiple_of(at * TILE, TILE))
            return carry

        lax.fori_loop(0, SEQ // TILE, step, 0)


    def norm_one(at):
        normed, _ = normalize(tok[pl.ds(at, TILE), :].astype(f32))
        H1[pl.ds(pl.multiple_of(q * SEQ + at, TILE), TILE), :] = (
            normed * (1.0 + row_of(1)) + row_of(0)
        ).astype(bf16)

    tiles(norm_one)

    def spread_start(buf, ident):
        part = buf.at[slot_rows(q), :]
        send(part, part, ident, mate)
        send(part, part, ident + 1, xnb)

    def spread_mid(buf, ident):
        part = buf.at[slot_rows(qx_), :]
        got(part, ident + 1)
        send(part, part, ident + 2, mate)

    def spread_mate(buf, ident):
        got(buf.at[slot_rows(qp_), :], ident)

    def spread_end(buf, ident):
        got(buf.at[slot_rows(qd_), :], ident + 2)

    spread_start(H1, IDS.h1)
    settle(tuple(IDS.core))

    def add_row(at, value):
        acc[at : at + 1, :] += jnp.sum(value, axis=0, keepdims=True)

    def out_gate(at):
        low = (og[pl.ds(at, TILE), :].astype(f32) * row_of(5)).astype(bf16)
        D2[pl.ds(pl.multiple_of(q * SEQ + at, TILE), TILE), :] = low
        add_row(6, low.astype(f32))

    tiles(out_gate)
    spread_start(D2, IDS.d2)
    spread_mate(H1, IDS.h1)
    forward(0, 3)
    forward(0, 2)
    spread_mid(H1, IDS.h1)
    arrived(0)


    def project(slot):
        rows = slot_rows(slot)
        value = (dot_nn(H1[rows, :], G_qkv[...]) + bias[3:4, :QKV]).astype(bf16)
        blank = jnp.zeros((SEQ, PAD - HEAD_DIM), bf16)
        for at in range(12):
            qp[rows, at * PAD : (at + 1) * PAD] = jnp.concatenate(
                [value[:, at * HEAD_DIM : (at + 1) * HEAD_DIM], blank], axis=1
            )

    def attend(slot):
        rows = slot_rows(slot)
        where_seg = slot_of(lax.rem(slot, 2), lax.div(slot, 2), y, z)
        seg = S[where_seg, 5:6, :SEQ]
        seg_column = jnp.transpose(jnp.broadcast_to(seg, (8, SEQ)))[:, :1]
        same = seg_column == seg
        pieces = []
        for head in range(LOCAL):
            query = qp[rows, head * PAD : (head + 1) * PAD]
            key = qp[rows, (LOCAL + head) * PAD : (LOCAL + head + 1) * PAD]
            value = qp[rows, (2 * LOCAL + head) * PAD : (2 * LOCAL + head + 1) * PAD]
            scores = jnp.where(same, dot_nt(query, key) * HEAD_DIM ** (-0.5), masked_score)
            exp_scores = jnp.exp(scores - jnp.max(scores, axis=1, keepdims=True))
            probs = (exp_scores / jnp.sum(exp_scores, axis=1, keepdims=True)).astype(bf16)
            P[slot * LOCAL + head] = probs
            pieces.append(dot_nn(probs, value).astype(bf16)[:, :HEAD_DIM])
        mixed[rows, :] = jnp.concatenate(pieces, axis=1)

    def pair(body, group):
        def step(at, carry):
            body(2 * group + lax.rem(c + at, 2))
            return carry

        lax.fori_loop(0, 2, step, 0)

    got(eight(1 - c, 1 - x), IDS.small_d)
    pair(project, x)
    pair(attend, x)
    proj_forward(1)
    spread_end(H1, IDS.h1)
    pair(project, 1 - x)
    proj_forward(3)
    pair(attend, 1 - x)
    proj_forward(2)
    forward(1, 1)
    spread_mate(D2, IDS.d2)
    spread_mid(D2, IDS.d2)


    def reduce_first(partial, rr, ident):
        sA[...] = partial(qd_).astype(bf16)
        send(sA, rr.at[0], ident, mate)
        keep[...] = partial(qx_)
        sB[...] = partial(qp_).astype(bf16)

    def reduce_next(partial, rr, ident):
        got(rr.at[0], ident)
        sX[...] = (keep[...] + rr[0].astype(f32)).astype(bf16)
        send(sX, rr.at[2], ident + 2, xnb)
        send(sB, rr.at[1], ident + 1, mate)
        own[...] = partial(q)

    def reduce_last(rr, ident):
        got(rr.at[1], ident + 1)
        got(rr.at[2], ident + 2)
        settle((ident, ident + 1, ident + 2))

    def total_rows(rr, at):
        rows = pl.ds(at, TILE)
        return own[rows, :] + rr[1, rows, :].astype(f32) + rr[2, rows, :].astype(f32)

    proj_arrived()

    def part_one(slot):
        return dot_nn(mixed[slot_rows(slot), :], W_proj[...])

    reduce_first(part_one, rrA, IDS.r1)
    reduce_next(part_one, rrA, IDS.r1)
    forward(1, 3)
    own_y(2)
    reduce_last(rrA, IDS.r1)


    def norm_two(at):
        rows = pl.ds(at, TILE)
        branch = total_rows(rrA, at) + bias[0:1, :]
        b1[rows, :] = branch
        stream = tok[rows, :].astype(f32) + row_of(2) * branch
        resid[rows, :] = stream
        normed, _ = normalize(stream)
        H2[pl.ds(pl.multiple_of(q * SEQ + at, TILE), TILE), :] = (
            normed * (1.0 + row_of(4)) + row_of(3)
        ).astype(bf16)

    tiles(norm_two)
    spread_start(H2, IDS.h2)
    forward(1, 2)
    spread_end(D2, IDS.d2)
    spread_mate(H2, IDS.h2)
    spread_mid(H2, IDS.h2)
    arrived(1)

    CHUNK = 384

    def first_layer(slot):
        rows = slot_rows(slot)
        for at in range(0, PART, CHUNK):
            pre = dot_nn(H2[rows, :], G_fc1[:, at : at + CHUNK]) + bias[2:3, at : at + CHUNK]
            square = pre * pre
            bend = jnp.tanh(root_half * (pre + 0.044715 * square * pre))
            active[rows, at : at + CHUNK] = (0.5 * pre * (1.0 + bend)).astype(bf16)
            slope[rows, at : at + CHUNK] = (
                0.5 * (1.0 + bend)
                + 0.5 * pre * (1.0 - bend * bend) * root_half * (1.0 + 3.0 * 0.044715 * square)
            ).astype(bf16)

    pair(first_layer, x)
    forward(2, 1)
    spread_end(H2, IDS.h2)
    pair(first_layer, 1 - x)
    forward(2, 3)

    def cross(left, right, dest, width):
        def step(at, carry):
            part = pl.ds(pl.multiple_of(at * CHUNK, CHUNK), CHUNK)
            dest[part, :] = dot_tn(left[:, part], right[...]).astype(bf16)
            return carry

        lax.fori_loop(0, width // CHUNK, step, 0)

    cross(active, D2, g_fc2, PART)

    def grad_start(kind, grads, steps):
        for k in steps:
            send(
                grads.at[chip_rows(z_to(k), 1 - y), :], yr_w[kind].at[k], IDS.gy[kind] + k, ynb
            )

    def add_block(grads, rows_at, extra):
        def step(at, carry):
            rows = pl.ds(pl.multiple_of(rows_at + at * 48, 16), 48)
            grads[rows, :] = (
                grads[rows, :].astype(f32) + extra[pl.ds(pl.multiple_of(at * 48, 16), 48), :].astype(f32)
            ).astype(bf16)
            return carry

        lax.fori_loop(0, 3, step, 0)

    def grad_mid(kind, grads, k):
        zz = z_to(k)
        got(yr_w[kind].at[k], IDS.gy[kind] + k)
        add_block(grads, (2 * zz + y) * 144, yr_w[kind].at[k])
        send(
            grads.at[chip_rows(zz, y), :], zr_w[kind].at[k - 1], IDS.gz[kind] + k - 1, znb(k)
        )

    def grad_end(kind, grads):
        got(yr_w[kind].at[0], IDS.gy[kind])
        for k in (1, 2, 3):
            got(zr_w[kind].at[k - 1], IDS.gz[kind] + k - 1)
        width = grads.shape[1]
        A, B, fr = fa_w[kind], fb_w[kind], fr_w[kind]
        for at in range(0, width, CHUNK):
            cols = slice(at, min(at + CHUNK, width))
            total = grads[chip_rows(z, y), cols].astype(f32) + yr_w[kind][0, :, cols].astype(f32)
            for k in range(3):
                total = total + zr_w[kind][k, :, cols].astype(f32)
            low, high = total[:72], total[72:]
            mine = jnp.where(c == 0, low, high).astype(bf16)
            A[:, cols] = mine
            B[:, cols] = jnp.where(c == 0, high, low).astype(bf16)
            fr[q, :, cols] = mine
        send(B, fr.at[q], IDS.gf[kind], mate)
        send(A, fr.at[q], IDS.gf[kind] + 1, xnb)
        send(B, fr.at[q], IDS.gf[kind] + 2, diag)

    slots = [area.at[72 * at : 72 * (at + 1), :] for area in (resid, b1, keep, own) for at in range(3)]
    out_copies = []

    def leave(value, target):
        at = len(out_copies)
        if at >= len(slots):
            out_copies[at - len(slots)].wait()
        slots[at % len(slots)][...] = value
        copy = pltpu.make_async_copy(slots[at % len(slots)], target, loc.at[2 + at])
        copy.start()
        out_copies.append(copy)

    def columns_of(ref, piece):
        return ref.at[:, piece * WIDTH : (piece + 1) * WIDTH]

    def grad_out(kind):
        fr = fr_w[kind]
        for step, source in enumerate((qp_, qx_, qd_)):
            got(fr.at[source], IDS.gf[kind] + step)
        if kind == 2:
            for at in range(4):
                leave(fr[at].astype(f32), ofc2.at[at])
            return
        for piece in range(3 if kind == 0 else 4):
            leave(
                jnp.concatenate(
                    [
                        fr[at, :, (4 * piece + step) * 72 : (4 * piece + step + 1) * 72]
                        for step in range(4)
                        for at in range(4)
                    ],
                    axis=1,
                ).astype(f32),
                columns_of(oqkv if kind == 0 else ofc1, piece),
            )

    grad_start(2, g_fc2, (1,))
    forward(2, 2)
    grad_start(2, g_fc2, (3, 2, 0))
    arrived(2)

    def back_hidden(slot):
        rows = slot_rows(slot)
        for at in range(0, PART, CHUNK):
            low = (
                dot_nt(D2[rows, :], G_fc2[at : at + CHUNK, :])
                * slope[rows, at : at + CHUNK].astype(f32)
            ).astype(bf16)
            slope[rows, at : at + CHUNK] = low
            acc[8:9, at : at + CHUNK] += jnp.sum(low.astype(f32), axis=0, keepdims=True)

    pair(back_hidden, x)
    pair(back_hidden, 1 - x)
    d_pre = slope
    settle(tuple(IDS.d2 + step for step in range(3)))
    D1 = D2
    def part_three(slot):
        return dot_nt(d_pre[slot_rows(slot), :], G_fc1[...])

    reduce_first(part_three, rrA, IDS.r3)
    reduce_next(part_three, rrA, IDS.r3)
    cross(H2, d_pre, g_fc1, WIDTH)
    grad_start(1, g_fc1, (1, 3, 2, 0))
    grad_mid(2, g_fc2, 1)
    reduce_last(rrA, IDS.r3)

    def back_two(at):
        rows = pl.ds(at, TILE)
        d_hidden = total_rows(rrA, at)
        normed, inv = normalize(resid[rows, :])
        add_row(3, d_hidden)
        add_row(4, d_hidden * normed)
        d_resid = og[rows, :].astype(f32) + normalize_back(d_hidden * (1.0 + row_of(4)), normed, inv)
        add_row(2, d_resid * b1[rows, :])
        low = (d_resid * row_of(2)).astype(bf16)
        add_row(7, low.astype(f32))
        D1[pl.ds(pl.multiple_of(q * SEQ + at, TILE), TILE), :] = low
        b1[rows, :] = d_resid

    tiles(back_two)
    spread_start(D1, IDS.d1)

    def part_two(slot):
        return dot_nn(active[slot_rows(slot), :], G_fc2[...])

    reduce_first(part_two, rrB, IDS.r2)
    reduce_next(part_two, rrB, IDS.r2)

    def finish_forward(at):
        rows = pl.ds(at, TILE)
        branch = total_rows(rrB, at) + bias[1:2, :]
        rrB[0, rows, :] = (resid[rows, :] + row_of(5) * branch).astype(bf16)
        add_row(5, og[rows, :].astype(f32) * branch)

    grad_mid(2, g_fc2, 3)
    spread_mate(D1, IDS.d1)


    def attend_backward(slot):
        rows = slot_rows(slot)
        d_mix = dot_nt(D1[rows, :], W_proj[...]).astype(bf16)
        blank = jnp.zeros((SEQ, PAD - HEAD_DIM), bf16)
        scale = HEAD_DIM ** (-0.5)
        d_query, d_key, d_value = [], [], []
        for head in range(LOCAL):
            query = qp[rows, head * PAD : (head + 1) * PAD]
            key = qp[rows, (LOCAL + head) * PAD : (LOCAL + head + 1) * PAD]
            value = qp[rows, (2 * LOCAL + head) * PAD : (2 * LOCAL + head + 1) * PAD]
            d_head = jnp.concatenate([d_mix[:, head * HEAD_DIM : (head + 1) * HEAD_DIM], blank], axis=1)
            probs = P[slot * LOCAL + head]
            d_probs = dot_nt(d_head, value)
            d_value.append(dot_tn(probs, d_head).astype(bf16)[:, :HEAD_DIM])
            wide = probs.astype(f32)
            d_scores = (wide * (d_probs - jnp.sum(d_probs * wide, axis=1, keepdims=True))).astype(bf16)
            d_query.append((dot_nn(d_scores, key) * scale).astype(bf16)[:, :HEAD_DIM])
            d_key.append((dot_tn(d_scores, query) * scale).astype(bf16)[:, :HEAD_DIM])
        value = jnp.concatenate(d_query + d_key + d_value, axis=1)
        dprj[rows, :] = value
        acc[9:10, :QKV] += jnp.sum(value.astype(f32), axis=0, keepdims=True)

    pair(attend_backward, x)
    spread_mid(D1, IDS.d1)
    grad_mid(2, g_fc2, 2)
    spread_end(D1, IDS.d1)
    pair(attend_backward, 1 - x)
    cross(H1, dprj, g_qkv, WIDTH)
    grad_start(0, g_qkv, (1, 3, 2, 0))
    grad_mid(1, g_fc1, 1)
    proj_grads = dot_tn(mixed[...], D1[...])
    for head in range(LOCAL):
        g_proj[head] = proj_grads[head * 72 : (head + 1) * 72].astype(bf16)

    @pl.when(jnp.logical_not(in_column))
    def _():
        for k in range(4):
            rc(g_proj.at[z_to(k)], yr_proj.at[k], IDS.gy[3] + k, ynb).start()

    def part_four(slot):
        return dot_nt(dprj[slot_rows(slot), :], G_qkv[...])

    settle((IDS.r2, IDS.r2 + 1))
    reduce_first(part_four, rrA, IDS.r4)
    reduce_last(rrB, IDS.r2)
    tiles(finish_forward)
    row_copies = [pltpu.make_async_copy(rrB.at[0], out, loc.at[20])]
    row_copies[0].start()
    reduce_next(part_four, rrA, IDS.r4)
    grad_mid(1, g_fc1, 3)
    grad_mid(1, g_fc1, 2)
    grad_end(2, g_fc2)
    reduce_last(rrA, IDS.r4)

    def back_one(at):
        rows = pl.ds(at, TILE)
        d_hidden = total_rows(rrA, at)
        normed, inv = normalize(tok[rows, :].astype(f32))
        add_row(0, d_hidden)
        add_row(1, d_hidden * normed)
        sA[rows, :] = (
            b1[rows, :] + normalize_back(d_hidden * (1.0 + row_of(1)), normed, inv)
        ).astype(bf16)

    tiles(back_one)
    row_copies.append(pltpu.make_async_copy(sA, tgrad, loc.at[21]))
    row_copies[1].start()

    E[my_slot] = acc[...].astype(bf16)
    send(E.at[my_slot], E.at[my_slot], IDS.end_y, ynb)

    @pl.when(in_column)
    def _():
        for k in STEPS:
            zz = z_to(k)
            got(yr_proj.at[k], IDS.gy[3] + k)
            g_proj[zz] = (g_proj[zz].astype(f32) + yr_proj[k].astype(f32)).astype(bf16)
            rc(g_proj.at[zz], zr_proj.at[k - 1], IDS.gz[3] + k - 1, znb(k)).start()

    got(E.at[slot_of(c, x, 1 - y, z)], IDS.end_y)
    for k in (2, 1, 3):
        for yy in range(2):
            part = E.at[slot_of(c, x, yy, z)]
            send(part, part, IDS.end_z + 2 * (k - 1) + yy, znb(k))
    for k in STEPS:
        grad_mid(0, g_qkv, k)
    for k in (1, 2, 3):
        for yy in range(2):
            got(E.at[slot_of(c, x, yy, z_from(k))], IDS.end_z + 2 * (k - 1) + yy)
    group = lambda cc, xx: E.at[pl.ds((cc * 2 + xx) * 8, 8)]
    send(group(c, x), group(c, x), IDS.end_x, xnb)
    grad_end(1, g_fc1)

    @pl.when(in_column)
    def _():
        got(yr_proj.at[0], IDS.gy[3])
        total = g_proj[z].astype(f32) + yr_proj[0].astype(f32)
        for k in (1, 2, 3):
            got(zr_proj.at[k - 1], IDS.gz[3] + k - 1)
            total = total + zr_proj[k - 1].astype(f32)
        p_out[...] = total.astype(bf16)
        rc(p_out, p_out, IDS.gf[3], xnb).start()

    got(group(c, 1 - x), IDS.end_x)
    send(E.at[pl.ds(c * 16, 16)], E.at[pl.ds(c * 16, 16)], IDS.end_c, mate)
    grad_out(2)

    @pl.when(jnp.logical_not(in_column))
    def _():
        got(p_out, IDS.gf[3])

    leave(p_out[...].astype(f32), oproj)
    got(E.at[pl.ds((1 - c) * 16, 16)], IDS.end_c)

    act_all = pick_columns(lambda piece: S[:, piece, :].astype(bf16))[:, :72]
    for section in range(6):
        rows = E[:, section, :]
        leave(dot_tn(act_all, rows), columns_of(oada, section))
        osum[section : section + 1, :] = jnp.sum(rows.astype(f32), axis=0, keepdims=True)
    for section in (6, 7):
        osum[section : section + 1, :] = jnp.sum(E[:, section, :].astype(f32), axis=0, keepdims=True)
    for section in (8, 9):
        for quarter in range(4):
            start = ((quarter % 2) * 2 + quarter // 2) * 8
            at = 8 + 4 * (section - 8) + quarter
            osum[at : at + 1, :] = jnp.sum(
                E[start : start + 8, section, :].astype(f32), axis=0, keepdims=True
            )
    grad_out(1)
    grad_end(0, g_qkv)
    grad_out(0)
    for copy in out_copies[-len(slots) :]:
        copy.wait()
    for copy in row_copies:
        copy.wait()
    for src, ident, _ in pending:
        sent(src, ident)

    @pl.when(in_column)
    def _():
        for k in (1, 2, 3):
            sent(p_out, IDS.gz[3] + k - 1)
        sent(p_out, IDS.gf[3])

    @pl.when(jnp.logical_not(in_column))
    def _():
        for k in range(4):
            sent(p_out, IDS.gy[3] + k)


def one_kernel(
    tokens,
    cond,
    segment_ids,
    ada_weight,
    ada_bias,
    qkv_weight,
    qv_bias,
    proj_weight,
    proj_bias,
    fc1_weight,
    fc1_bias,
    fc2_weight,
    fc2_bias,
    out_grad,
):
    fsdp_at = lax.axis_index("fsdp")
    cond_float = cond[0].astype(f32)
    cond_act = (cond_float / (1.0 + jnp.exp(-cond_float))).astype(bf16).astype(f32)
    blank = lambda count: jnp.zeros((count,), f32)
    small = jnp.concatenate(
        [
            cond_act,
            qv_bias.astype(f32),
            proj_bias.astype(f32),
            fc2_bias.astype(f32),
            blank(96),
            fc1_bias.astype(f32),
            blank(96),
            segment_ids[0].astype(f32),
            blank(128 + 768),
        ]
    ).reshape(8, 384)
    adab = lax.dynamic_update_slice_in_dim(
        blank(8 * WIDTH), ada_bias.astype(f32), fsdp_at * 432, 0
    ).reshape(8, WIDTH)
    wfc2 = fc2_weight.reshape(4, 72, WIDTH)
    vmem = pl.BlockSpec(memory_space=pltpu.VMEM)
    anywhere = pl.BlockSpec(memory_space=pl.ANY)
    outside = pl.BlockSpec(memory_space=pltpu.HBM)
    shape = jax.ShapeDtypeStruct
    scratch = [pltpu.VMEM(dims, kind) for dims, kind in SCRATCH]
    out, tgrad, oada, oqkv, oproj, ofc1, ofc2, osum = pl.pallas_call(
        block_kernel,
        out_shape=(
            shape((SEQ, WIDTH), bf16),
            shape((SEQ, WIDTH), bf16),
            shape((72, 6 * WIDTH), f32),
            shape((72, 3 * WIDTH), f32),
            shape((72, WIDTH), f32),
            shape((72, HIDDEN), f32),
            shape((4, 72, WIDTH), f32),
            shape((16, WIDTH), f32),
        ),
        in_specs=[vmem, vmem, vmem, vmem, vmem, vmem, anywhere, vmem, anywhere],
        out_specs=(outside,) * 7 + (vmem,),
        scratch_shapes=scratch
        + [
            pltpu.SemaphoreType.DMA((ID_COUNT,)),
            pltpu.SemaphoreType.DMA((ID_COUNT,)),
            pltpu.SemaphoreType.DMA((22,)),
        ],
        compiler_params=pltpu.CompilerParams(
            collective_id=0, has_side_effects=True, vmem_limit_bytes=67043328
        ),
        name="whole_block",
    )(tokens[0], out_grad[0], small, ada_weight, adab, qkv_weight, proj_weight, fc1_weight, wfc2)
    def mine(vector, count):
        return lax.dynamic_slice_in_dim(vector, fsdp_at * count, count, 0)

    by_head = osum[12:16, :QKV].reshape(4, 3, 4, 72).transpose(1, 2, 0, 3).reshape(3 * WIDTH)
    return (
        out[None],
        tgrad[None],
        oada,
        mine(osum[:6].reshape(-1), 432),
        oqkv,
        mine(jnp.concatenate([by_head[:WIDTH], by_head[2 * WIDTH :]]), 144),
        oproj,
        mine(osum[7], 72),
        ofc1,
        mine(osum[8:12].reshape(4, 16, 72).transpose(1, 0, 2).reshape(-1), 288),
        ofc2.reshape(288, WIDTH),
        mine(osum[6], 72),
    )


def solution(mesh):
    in_specs = (
        P(("fsdp", "dp"), None, None),
        P(("fsdp", "dp"), None),
        P(("fsdp", "dp"), None),
        P("fsdp", None),
        P("fsdp"),
        P("fsdp", None),
        P("fsdp"),
        P("fsdp", None),
        P("fsdp"),
        P("fsdp", None),
        P("fsdp"),
        P("fsdp", None),
        P("fsdp"),
        P(("fsdp", "dp"), None, None),
    )
    out_specs = (
        P(("fsdp", "dp"), None, None),
        P(("fsdp", "dp"), None, None),
        P("fsdp", None),
        P("fsdp"),
        P("fsdp", None),
        P("fsdp"),
        P("fsdp", None),
        P("fsdp"),
        P("fsdp", None),
        P("fsdp"),
        P("fsdp", None),
        P("fsdp"),
    )
    fits = (mesh.shape["fsdp"], mesh.shape["dp"]) == (16, 2)
    return jax.shard_map(
        one_kernel if fits else general_form, mesh=mesh, in_specs=in_specs, out_specs=out_specs, check_vma=False
    )
```

profile of v0, /device:TPU:0, one launch (start us, length us, event | category | flops | bytes accessed | tf_op | source)
XLA Modules:
  0.0 318.2 jit_solution(17874982754792570511)
XLA Ops:
  0.6 0.7 convert_element_type.41
  1.3 0.7 convert_reduce_fusion
  2.1 2.8 concatenate.6
  4.8 0.6 reshape.56.small
  5.5 0.8 convert_dynamic-update-slice_fusion
  6.2 0.6 reshape.57.adab
  6.8 295.5 %whole_block.1 = (bf16[256,1152]{1,0:T(8,128)(2,1)}, bf16[256,1152]{1,0:T(8,128)(2,1)}, f32[72,6912]{1,0:T(8,128)}, f32[72,3456]{1,0:T(8,128)}, f32[72,1152]{1,0...) custom-call(bf16[256,1152]{1,0:T(8,128)(2,1)} %bitcast.19, bf16[256,1152]{1,0:T(8,128)(2,1)} %bitcast.20, ...), custom_call_target="tpu_custom_call" | custom-call | tf_op jit(solution)/shard_map/whole_block/pallas_call | solution.py:1234
  302.4 0.0 copy-start.4
  302.4 0.9 fusion.2
  303.2 0.6 dynamic-slice_bitcast_fusion
  303.8 0.8 slice.28
  304.6 0.1 reshape.60
  304.7 0.1 slice.32
  304.8 0.1 slice.30
  304.9 0.7 fusion.1
  305.5 0.8 slice.34
  306.3 0.9 slice.27
  307.2 0.7 dynamic_slice.19
  307.9 0.1 reshape.61
  308.0 0.1 reshape.62
  308.1 0.7 dynamic_slice.23
  308.8 1.9 copy.40
  310.7 0.0 copy-done.4
  310.7 0.8 copy.41
  311.5 1.3 copy.42
  312.8 0.6 copy-done.3
  313.4 0.9 copy.43
  314.4 0.2 copy-done.5
  314.6 0.7 copy.44
  315.3 1.1 copy.45
  316.4 0.7 copy-done.1
  317.1 1.1 copy.46
  (15 shorter events, 0.1 us)
Async XLA Ops:
  302.4 8.3 %copy-start.4 = (bf16[256,1152]{1,0:T(8,128)(2,1)S(1)}, bf16[256,1152]{1,0:T(8,128)(2,1)}, u32[]{:S(2)}) copy-start(bf16[256,1152]{1,0:T(8,128)(2,1)} %get-tuple-element.21) | copy-start | bytes 1769476
  306.3 5.2 %copy-start = (f32[72,6912]{1,0:T(8,128)S(1)}, f32[72,6912]{1,0:T(8,128)}, u32[]{:S(2)}) copy-start(f32[72,6912]{1,0:T(8,128)} %get-tuple-element.48) | copy-start | bytes 5971972
  311.5 1.9 copy-start.3
  313.4 1.2 copy-start.5
  313.4 1.9 copy-start.2
  315.3 1.8 copy-start.1
where the time goes:
time: 319 us; the launch traced here: 318 us
  Pallas kernels  296 us (93%)
  local copies, waits for them, and re-layouts  19.1 us (6%)
    pallas_call x1, Pallas kernels, one_kernel(): pl.pallas_call(block_kernel, out_shape=(shape((SEQ, WIDTH), bf16), shape(...  296 us
    unnamed x19, local copies, waits for them, and re-layouts  9.41 us

commit v1 on v0

--- a/solution.py
+++ b/solution.py
@@ -622,7 +622,6 @@
     eight = lambda cc, xx: S.at[pl.ds((cc * 2 + xx) * 8, 8)]
     send(eight(c, x), eight(c, x), IDS.small_c, mate)
     send(eight(c, x), eight(c, x), IDS.small_x, xnb)
-    split_fc1()
 
     def pick_columns(rows):
         total = None
@@ -635,6 +634,7 @@
         return total.astype(bf16)
 
     got(eight(1 - c, x), IDS.small_c)
+    own_z(0, (2,))
     act = pick_columns(
         lambda piece: jnp.concatenate(
             [S[pl.ds((cc * 2 + x) * 8, 8), piece, :] for cc in range(2)], axis=0
@@ -648,23 +648,23 @@
         modp[:, section, :] = jnp.zeros((16, WIDTH), f32)
     theirs, ours = modp.at[pl.ds((1 - c) * 8, 8)], modp.at[pl.ds(c * 8, 8)]
     send(theirs, modc, IDS.mod_c, mate)
-    own_copy.wait()
-    assemble(1)
-    assemble(2)
+    split_fc1()
     got(modc, IDS.mod_c)
     for at in range(8):
         ours[at] += modc[at]
     send(modp.at[pl.ds(c * 8 + (1 - y) * 4, 4)], mody, IDS.mod_y, ynb)
     forward(0, 1)
+    own_copy.wait()
+    assemble(1)
     got(mody, IDS.mod_y)
     base = c * 8 + y * 4
     for at in range(4):
         modp[base + at] += mody[at]
     for k in (2, 1, 3):
         send(modp.at[base + z_to(k)], modz.at[k - 1], IDS.mod_z + k - 1, znb(k))
-    own_z(0, (2,))
     proj_z()
     own_z(1, STEPS)
+    assemble(2)
     own_z(2, STEPS)
     proj_y()
     own_y(1)
@@ -1064,33 +1064,30 @@
     pair(attend_backward, x)
     spread_mid(D1, IDS.d1)
     grad_mid(2, g_fc2, 2)
+    grad_mid(1, g_fc1, 1)
     spread_end(D1, IDS.d1)
     pair(attend_backward, 1 - x)
+    grad_mid(1, g_fc1, 3)
     cross(H1, dprj, g_qkv, WIDTH)
     grad_start(0, g_qkv, (1, 3, 2, 0))
-    grad_mid(1, g_fc1, 1)
-    proj_grads = dot_tn(mixed[...], D1[...])
-    for head in range(LOCAL):
-        g_proj[head] = proj_grads[head * 72 : (head + 1) * 72].astype(bf16)
-
-    @pl.when(jnp.logical_not(in_column))
-    def _():
-        for k in range(4):
-            rc(g_proj.at[z_to(k)], yr_proj.at[k], IDS.gy[3] + k, ynb).start()
 
     def part_four(slot):
         return dot_nt(dprj[slot_rows(slot), :], G_qkv[...])
 
     settle((IDS.r2, IDS.r2 + 1))
     reduce_first(part_four, rrA, IDS.r4)
+    grad_mid(1, g_fc1, 2)
     reduce_last(rrB, IDS.r2)
     tiles(finish_forward)
     row_copies = [pltpu.make_async_copy(rrB.at[0], out, loc.at[20])]
     row_copies[0].start()
     reduce_next(part_four, rrA, IDS.r4)
-    grad_mid(1, g_fc1, 3)
-    grad_mid(1, g_fc1, 2)
+    proj_grads = dot_tn(mixed[...], D1[...])
+    for head in range(LOCAL):
+        g_proj[head] = proj_grads[head * 72 : (head + 1) * 72].astype(bf16)
+    grad_mid(0, g_qkv, 1)
     grad_end(2, g_fc2)
+    grad_mid(0, g_qkv, 3)
     reduce_last(rrA, IDS.r4)
 
     def back_one(at):
@@ -1110,6 +1107,19 @@
     E[my_slot] = acc[...].astype(bf16)
     send(E.at[my_slot], E.at[my_slot], IDS.end_y, ynb)
 
+    @pl.when(jnp.logical_not(in_column))
+    def _():
+        for k in range(4):
+            rc(g_proj.at[z_to(k)], yr_proj.at[k], IDS.gy[3] + k, ynb).start()
+
+    grad_mid(0, g_qkv, 2)
+    grad_end(1, g_fc1)
+    got(E.at[slot_of(c, x, 1 - y, z)], IDS.end_y)
+    for k in (2, 1, 3):
+        for yy in range(2):
+            part = E.at[slot_of(c, x, yy, z)]
+            send(part, part, IDS.end_z + 2 * (k - 1) + yy, znb(k))
+
     @pl.when(in_column)
     def _():
         for k in STEPS:
@@ -1118,19 +1128,13 @@
             g_proj[zz] = (g_proj[zz].astype(f32) + yr_proj[k].astype(f32)).astype(bf16)
             rc(g_proj.at[zz], zr_proj.at[k - 1], IDS.gz[3] + k - 1, znb(k)).start()
 
-    got(E.at[slot_of(c, x, 1 - y, z)], IDS.end_y)
-    for k in (2, 1, 3):
-        for yy in range(2):
-            part = E.at[slot_of(c, x, yy, z)]
-            send(part, part, IDS.end_z + 2 * (k - 1) + yy, znb(k))
-    for k in STEPS:
-        grad_mid(0, g_qkv, k)
+    grad_out(2)
     for k in (1, 2, 3):
         for yy in range(2):
             got(E.at[slot_of(c, x, yy, z_from(k))], IDS.end_z + 2 * (k - 1) + yy)
     group = lambda cc, xx: E.at[pl.ds((cc * 2 + xx) * 8, 8)]
     send(group(c, x), group(c, x), IDS.end_x, xnb)
-    grad_end(1, g_fc1)
+    grad_end(0, g_qkv)
 
     @pl.when(in_column)
     def _():
@@ -1142,9 +1146,9 @@
         p_out[...] = total.astype(bf16)
         rc(p_out, p_out, IDS.gf[3], xnb).start()
 
+    grad_out(1)
     got(group(c, 1 - x), IDS.end_x)
     send(E.at[pl.ds(c * 16, 16)], E.at[pl.ds(c * 16, 16)], IDS.end_c, mate)
-    grad_out(2)
 
     @pl.when(jnp.logical_not(in_column))
     def _():
@@ -1167,8 +1171,6 @@
             osum[at : at + 1, :] = jnp.sum(
                 E[start : start + 8, section, :].astype(f32), axis=0, keepdims=True
             )
-    grad_out(1)
-    grad_end(0, g_qkv)
     grad_out(0)
     for copy in out_copies[-len(slots) :]:
         copy.wait()

time: 319 us -> 311 us (0.975); the launches traced: 318 us -> 306 us
  Pallas kernels: 296 us -> 284 us
    pallas_call x1, Pallas kernels: 296 us -> 284 us  [one_kernel(): pl.pallas_call(block_kernel, out_shape=(shape((SEQ, WIDTH), bf16), shape(...]
where the time goes in v1:
time: 311 us; the launch traced here: 306 us
  Pallas kernels  284 us (91%)
  local copies, waits for them, and re-layouts  19.1 us (6%)
    pallas_call x1, Pallas kernels, one_kernel(): pl.pallas_call(block_kernel, out_shape=(shape((SEQ, WIDTH), bf16), shape(...  284 us
    unnamed x19, local copies, waits for them, and re-layouts  9.41 us

profile of v1, /device:TPU:0, one launch (start us, length us, event | category | flops | bytes accessed | tf_op | source)
XLA Modules:
  0.0 306.5 jit_solution(9581090388838342156)
XLA Ops:
  0.6 0.7 convert_element_type.41
  1.3 0.7 convert_reduce_fusion
  2.1 2.8 concatenate.6
  4.8 0.6 reshape.56.small
  5.5 0.8 convert_dynamic-update-slice_fusion
  6.2 0.6 reshape.57.adab
  6.8 283.8 %whole_block.1 = (bf16[256,1152]{1,0:T(8,128)(2,1)}, bf16[256,1152]{1,0:T(8,128)(2,1)}, f32[72,6912]{1,0:T(8,128)}, f32[72,3456]{1,0:T(8,128)}, f32[72,1152]{1,0...) custom-call(bf16[256,1152]{1,0:T(8,128)(2,1)} %bitcast.19, bf16[256,1152]{1,0:T(8,128)(2,1)} %bitcast.20, ...), custom_call_target="tpu_custom_call" | custom-call | tf_op jit(solution)/shard_map/whole_block/pallas_call | solution.py:1236
  290.7 0.0 copy-start.4
  290.7 0.9 fusion.2
  291.5 0.6 dynamic-slice_bitcast_fusion
  292.1 0.8 slice.28
  292.9 0.1 reshape.60
  293.0 0.1 slice.32
  293.1 0.1 slice.30
  293.2 0.7 fusion.1
  293.9 0.8 slice.34
  294.6 0.9 slice.27
  295.6 0.7 dynamic_slice.19
  296.2 0.1 reshape.61
  296.3 0.1 reshape.62
  296.4 0.7 dynamic_slice.23
  297.1 1.9 copy.40
  299.0 0.0 copy-done.4
  299.0 0.8 copy.41
  299.8 1.3 copy.42
  301.1 0.6 copy-done.3
  301.7 0.9 copy.43
  302.7 0.2 copy-done.5
  302.9 0.7 copy.44
  303.6 1.1 copy.45
  304.7 0.7 copy-done.1
  305.4 1.1 copy.46
  (15 shorter events, 0.1 us)
Async XLA Ops:
  290.7 8.3 %copy-start.4 = (bf16[256,1152]{1,0:T(8,128)(2,1)S(1)}, bf16[256,1152]{1,0:T(8,128)(2,1)}, u32[]{:S(2)}) copy-start(bf16[256,1152]{1,0:T(8,128)(2,1)} %get-tuple-element.21) | copy-start | bytes 1769476
  294.6 5.2 %copy-start = (f32[72,6912]{1,0:T(8,128)S(1)}, f32[72,6912]{1,0:T(8,128)}, u32[]{:S(2)}) copy-start(f32[72,6912]{1,0:T(8,128)} %get-tuple-element.48) | copy-start | bytes 5971972
  299.8 1.9 copy-start.3
  301.7 1.2 copy-start.5
  301.7 1.9 copy-start.2
  303.6 1.8 copy-start.1

commit v2 on v1

--- a/solution.py
+++ b/solution.py
@@ -367,6 +367,7 @@
 IDS.core = [IDS.take(1) for _ in range(3)]
 IDS.z = [IDS.take(3) for _ in range(4)]
 IDS.y = [IDS.take(4) for _ in range(4)]
+IDS.pass_on = [IDS.take(5) for _ in range(4)]
 IDS.h1, IDS.h2, IDS.d2, IDS.d1 = IDS.take(3), IDS.take(3), IDS.take(3), IDS.take(3)
 IDS.r1, IDS.r2, IDS.r3, IDS.r4 = IDS.take(3), IDS.take(3), IDS.take(3), IDS.take(3)
 IDS.gy = [IDS.take(4) for _ in range(4)]
@@ -552,57 +553,86 @@
     def own_y(kind):
         send(own_part(kind), own_part(kind), IDS.y[kind], ynb)
 
-    def own_z(kind, steps):
-        for k in steps:
-            send(own_part(kind), own_part(kind), IDS.z[kind] + k - 1, znb(k))
+    inner = (z == 1) | (z == 2)
+    relays = []
+
+    def relay(wanted, part, source, ident, send_ident, to):
+        @pl.when(wanted)
+        def _():
+            pltpu.make_async_remote_copy(
+                src_ref=source, dst_ref=part, send_sem=snd.at[send_ident], recv_sem=rcv.at[ident],
+                device_id=to, device_id_type=MESH_ID,
+            ).start()
+
+        relays.append((wanted, part, send_ident))
+
+    def own_z(kind):
+        part = own_part(kind)
+        relay(z < 3, part, part, IDS.z[kind], IDS.pass_on[kind], znb(1))
+        relay(z > 0, part, part, IDS.z[kind] + 2, IDS.pass_on[kind] + 1, znb(3))
 
     STEPS = (1, 3, 2)
 
-    def forward(kind, k):
+    def near(j):
+        middle = STEPS[j]
+        return jnp.where(z == 0, 3 - j, jnp.where(z == 3, 1 + j, middle))
+
+    def onward(k):
+        return lax.rem(z + jnp.where(k <= z, 1, 3), 4), jnp.where(k <= z, k, k - 2)
+
+    def forward(kind, j):
+        k = near(j)
         part = G_w[kind].at[chip_rows(z_from(k), y), :]
         got(part, IDS.z[kind] + k - 1)
-        send(part, part, IDS.y[kind] + k, ynb)
+        where, at = onward(k)
+        relay(inner, part, part, IDS.z[kind] + at, IDS.pass_on[kind] + 2 + j, dev(where, y, c, x))
+        send(part, part, IDS.y[kind] + 1 + j, ynb)
 
     def arrived(kind):
         other = 1 - y
         got(G_w[kind].at[chip_rows(z, other), :], IDS.y[kind])
-        for k in STEPS:
-            got(G_w[kind].at[chip_rows(z_from(k), other), :], IDS.y[kind] + k)
+        for j in range(3):
+            got(G_w[kind].at[chip_rows(z_from(near(j)), other), :], IDS.y[kind] + 1 + j)
 
     def proj_z():
         @pl.when(in_column)
         def _():
             proj_copy.start()
-            for k in STEPS:
-                rc(wproj, G_proj.at[z], IDS.z[3] + k - 1, znb(k)).start()
+
+        part = G_proj.at[z]
+        relay(in_column & (z < 3), part, wproj, IDS.z[3], IDS.pass_on[3], znb(1))
+        relay(in_column & (z > 0), part, wproj, IDS.z[3] + 2, IDS.pass_on[3] + 1, znb(3))
 
     def proj_y():
         @pl.when(in_column)
         def _():
             rc(wproj, G_proj.at[z], IDS.y[3], ynb).start()
 
-    def proj_forward(k):
+    def proj_forward(j):
+        k = near(j)
+        part = G_proj.at[z_from(k)]
+
         @pl.when(in_column)
         def _():
-            part = G_proj.at[z_from(k)]
             got(part, IDS.z[3] + k - 1)
-            rc(part, part, IDS.y[3] + k, ynb).start()
+            rc(part, part, IDS.y[3] + 1 + j, ynb).start()
+
+        where, at = onward(k)
+        relay(in_column & inner, part, part, IDS.z[3] + at, IDS.pass_on[3] + 2 + j, dev(where, y, c, x))
 
     def proj_arrived():
         @pl.when(in_column)
         def _():
             proj_copy.wait()
-            for k in (1, 2, 3):
-                sent(wproj, IDS.z[3] + k - 1)
             sent(wproj, IDS.y[3])
-            for k in STEPS:
-                sent(G_proj.at[z_from(k)], IDS.y[3] + k)
+            for j in range(3):
+                sent(G_proj.at[z_from(near(j))], IDS.y[3] + 1 + j)
 
         @pl.when(jnp.logical_not(in_column))
         def _():
             got(G_proj.at[z], IDS.y[3])
-            for k in STEPS:
-                got(G_proj.at[z_from(k)], IDS.y[3] + k)
+            for j in range(3):
+                got(G_proj.at[z_from(near(j))], IDS.y[3] + 1 + j)
 
         W_proj[...] = jnp.concatenate(
             [G_proj[head].astype(f32) for head in range(LOCAL)], axis=0
@@ -615,7 +645,7 @@
             send(part, part, IDS.small_z + 2 * (k - 1) + yy, znb(k))
     assemble(0)
     own_y(0)
-    own_z(0, (1, 3))
+    own_z(0)
     for k in (1, 2, 3):
         for yy in range(2):
             got(S.at[slot_of(c, x, yy, z_from(k))], IDS.small_z + 2 * (k - 1) + yy)
@@ -634,7 +664,6 @@
         return total.astype(bf16)
 
     got(eight(1 - c, x), IDS.small_c)
-    own_z(0, (2,))
     act = pick_columns(
         lambda piece: jnp.concatenate(
             [S[pl.ds((cc * 2 + x) * 8, 8), piece, :] for cc in range(2)], axis=0
@@ -653,7 +682,7 @@
     for at in range(8):
         ours[at] += modc[at]
     send(modp.at[pl.ds(c * 8 + (1 - y) * 4, 4)], mody, IDS.mod_y, ynb)
-    forward(0, 1)
+    forward(0, 0)
     own_copy.wait()
     assemble(1)
     got(mody, IDS.mod_y)
@@ -662,10 +691,10 @@
         modp[base + at] += mody[at]
     for k in (2, 1, 3):
         send(modp.at[base + z_to(k)], modz.at[k - 1], IDS.mod_z + k - 1, znb(k))
+    forward(0, 1)
     proj_z()
-    own_z(1, STEPS)
+    own_z(1)
     assemble(2)
-    own_z(2, STEPS)
     proj_y()
     own_y(1)
     got(eight(c, 1 - x), IDS.small_x)
@@ -760,7 +789,6 @@
     tiles(out_gate)
     spread_start(D2, IDS.d2)
     spread_mate(H1, IDS.h1)
-    forward(0, 3)
     forward(0, 2)
     spread_mid(H1, IDS.h1)
     arrived(0)
@@ -801,15 +829,18 @@
         lax.fori_loop(0, 2, step, 0)
 
     got(eight(1 - c, 1 - x), IDS.small_d)
+    proj_forward(0)
     pair(project, x)
+    forward(1, 0)
+    proj_forward(1)
     pair(attend, x)
-    proj_forward(1)
+    forward(1, 1)
+    proj_forward(2)
+    own_z(2)
     spread_end(H1, IDS.h1)
     pair(project, 1 - x)
-    proj_forward(3)
+    forward(1, 2)
     pair(attend, 1 - x)
-    proj_forward(2)
-    forward(1, 1)
     spread_mate(D2, IDS.d2)
     spread_mid(D2, IDS.d2)
 
@@ -843,8 +874,8 @@
 
     reduce_first(part_one, rrA, IDS.r1)
     reduce_next(part_one, rrA, IDS.r1)
-    forward(1, 3)
     own_y(2)
+    forward(2, 0)
     reduce_last(rrA, IDS.r1)
 
 
@@ -861,7 +892,7 @@
 
     tiles(norm_two)
     spread_start(H2, IDS.h2)
-    forward(1, 2)
+    forward(2, 1)
     spread_end(D2, IDS.d2)
     spread_mate(H2, IDS.h2)
     spread_mid(H2, IDS.h2)
@@ -882,10 +913,9 @@
             ).astype(bf16)
 
     pair(first_layer, x)
-    forward(2, 1)
+    forward(2, 2)
     spread_end(H2, IDS.h2)
     pair(first_layer, 1 - x)
-    forward(2, 3)
 
     def cross(left, right, dest, width):
         def step(at, carry):
@@ -977,9 +1007,7 @@
                 columns_of(oqkv if kind == 0 else ofc1, piece),
             )
 
-    grad_start(2, g_fc2, (1,))
-    forward(2, 2)
-    grad_start(2, g_fc2, (3, 2, 0))
+    grad_start(2, g_fc2, (1, 3, 2, 0))
     arrived(2)
 
     def back_hidden(slot):
@@ -1178,6 +1206,12 @@
         copy.wait()
     for src, ident, _ in pending:
         sent(src, ident)
+    for wanted, part, ident in relays:
+
+        @pl.when(wanted)
+        def _(part=part, ident=ident):
+            sent(part, ident)
+
 
     @pl.when(in_column)
     def _():

time: 311 us -> 288 us (0.926)
  the two profiles are of different devices: /device:TPU:0 before, /device:TPU:18 now
where the time goes in v2:
time: 288 us
  Pallas kernels  265 us (92%)
  local copies, waits for them, and re-layouts  19.1 us (7%)
    pallas_call x1, Pallas kernels, one_kernel(): pl.pallas_call(block_kernel, out_shape=(shape((SEQ, WIDTH), bf16), shape(...  265 us
    unnamed x19, local copies, waits for them, and re-layouts  9.41 us

profile of v2, /device:TPU:18, one launch (start us, length us, event | category | flops | bytes accessed | tf_op | source)
XLA Modules:
  0.0 287.7 jit_solution(16573796782483617828)
XLA Ops:
  0.6 0.7 convert_element_type.41
  1.3 0.7 convert_reduce_fusion
  2.1 2.8 concatenate.6
  4.8 0.6 reshape.56.small
  5.5 0.8 convert_dynamic-update-slice_fusion
  6.2 0.6 reshape.57.adab
  6.8 265.0 %whole_block.1 = (bf16[256,1152]{1,0:T(8,128)(2,1)}, bf16[256,1152]{1,0:T(8,128)(2,1)}, f32[72,6912]{1,0:T(8,128)}, f32[72,3456]{1,0:T(8,128)}, f32[72,1152]{1,0...) custom-call(bf16[256,1152]{1,0:T(8,128)(2,1)} %bitcast.19, bf16[256,1152]{1,0:T(8,128)(2,1)} %bitcast.20, ...), custom_call_target="tpu_custom_call" | custom-call | tf_op jit(solution)/shard_map/whole_block/pallas_call | solution.py:1270
  271.8 0.0 copy-start.4
  271.8 0.9 fusion.2
  272.7 0.6 dynamic-slice_bitcast_fusion
  273.3 0.8 slice.28
  274.1 0.1 reshape.60
  274.2 0.1 slice.32
  274.3 0.1 slice.30
  274.4 0.7 fusion.1
  275.0 0.8 slice.34
  275.8 0.9 slice.27
  276.7 0.7 dynamic_slice.19
  277.4 0.1 reshape.61
  277.5 0.1 reshape.62
  277.6 0.7 dynamic_slice.23
  278.2 1.9 copy.40
  280.2 0.8 copy.41
  281.0 0.0 copy-done
  281.0 1.3 copy.42
  282.3 0.6 copy-done.3
  282.9 0.9 copy.43
  283.9 0.2 copy-done.5
  284.1 0.7 copy.44
  284.8 1.1 copy.45
  285.9 0.7 copy-done.1
  286.6 1.1 copy.46
  (15 shorter events, 0.1 us)
Async XLA Ops:
  271.8 8.3 %copy-start.4 = (bf16[256,1152]{1,0:T(8,128)(2,1)S(1)}, bf16[256,1152]{1,0:T(8,128)(2,1)}, u32[]{:S(2)}) copy-start(bf16[256,1152]{1,0:T(8,128)(2,1)} %get-tuple-element.21) | copy-start | bytes 1769476
  275.8 5.2 %copy-start = (f32[72,6912]{1,0:T(8,128)S(1)}, f32[72,6912]{1,0:T(8,128)}, u32[]{:S(2)}) copy-start(f32[72,6912]{1,0:T(8,128)} %get-tuple-element.48) | copy-start | bytes 5971972
  281.0 1.9 copy-start.3
  282.9 1.2 copy-start.5
  282.9 1.9 copy-start.2
  284.8 1.8 copy-start.1

commit v3 on v2

--- a/solution.py
+++ b/solution.py
@@ -1007,7 +1007,7 @@
                 columns_of(oqkv if kind == 0 else ofc1, piece),
             )
 
-    grad_start(2, g_fc2, (1, 3, 2, 0))
+    grad_start(2, g_fc2, (2, 1, 3, 0))
     arrived(2)
 
     def back_hidden(slot):
@@ -1031,8 +1031,8 @@
     reduce_first(part_three, rrA, IDS.r3)
     reduce_next(part_three, rrA, IDS.r3)
     cross(H2, d_pre, g_fc1, WIDTH)
-    grad_start(1, g_fc1, (1, 3, 2, 0))
-    grad_mid(2, g_fc2, 1)
+    grad_start(1, g_fc1, (2, 1, 3, 0))
+    grad_mid(2, g_fc2, 2)
     reduce_last(rrA, IDS.r3)
 
     def back_two(at):
@@ -1063,7 +1063,7 @@
         rrB[0, rows, :] = (resid[rows, :] + row_of(5) * branch).astype(bf16)
         add_row(5, og[rows, :].astype(f32) * branch)
 
-    grad_mid(2, g_fc2, 3)
+    grad_mid(2, g_fc2, 1)
     spread_mate(D1, IDS.d1)
 
 
@@ -1091,20 +1091,20 @@
 
     pair(attend_backward, x)
     spread_mid(D1, IDS.d1)
-    grad_mid(2, g_fc2, 2)
-    grad_mid(1, g_fc1, 1)
+    grad_mid(2, g_fc2, 3)
+    grad_mid(1, g_fc1, 2)
     spread_end(D1, IDS.d1)
     pair(attend_backward, 1 - x)
-    grad_mid(1, g_fc1, 3)
+    grad_mid(1, g_fc1, 1)
     cross(H1, dprj, g_qkv, WIDTH)
-    grad_start(0, g_qkv, (1, 3, 2, 0))
+    grad_start(0, g_qkv, (2, 1, 3, 0))
 
     def part_four(slot):
         return dot_nt(dprj[slot_rows(slot), :], G_qkv[...])
 
     settle((IDS.r2, IDS.r2 + 1))
     reduce_first(part_four, rrA, IDS.r4)
-    grad_mid(1, g_fc1, 2)
+    grad_mid(1, g_fc1, 3)
     reduce_last(rrB, IDS.r2)
     tiles(finish_forward)
     row_copies = [pltpu.make_async_copy(rrB.at[0], out, loc.at[20])]
@@ -1113,9 +1113,9 @@
     proj_grads = dot_tn(mixed[...], D1[...])
     for head in range(LOCAL):
         g_proj[head] = proj_grads[head * 72 : (head + 1) * 72].astype(bf16)
+    grad_mid(0, g_qkv, 2)
+    grad_end(2, g_fc2)
     grad_mid(0, g_qkv, 1)
-    grad_end(2, g_fc2)
-    grad_mid(0, g_qkv, 3)
     reduce_last(rrA, IDS.r4)
 
     def back_one(at):
@@ -1140,7 +1140,7 @@
         for k in range(4):
             rc(g_proj.at[z_to(k)], yr_proj.at[k], IDS.gy[3] + k, ynb).start()
 
-    grad_mid(0, g_qkv, 2)
+    grad_mid(0, g_qkv, 3)
     grad_end(1, g_fc1)
     got(E.at[slot_of(c, x, 1 - y, z)], IDS.end_y)
     for k in (2, 1, 3):

time: 288 us -> 282 us (0.979)
  the two profiles are of different devices: /device:TPU:18 before, /device:TPU:0 now
where the time goes in v3:
time: 282 us; the launch traced here: 277 us
  Pallas kernels  254 us (90%)
  local copies, waits for them, and re-layouts  19.1 us (7%)
  other arithmetic  2.82 us (1%)
    pallas_call x1, Pallas kernels, one_kernel(): pl.pallas_call(block_kernel, out_shape=(shape((SEQ, WIDTH), bf16), shape(...  254 us
    unnamed x19, local copies, waits for them, and re-layouts  9.41 us

profile of v3, /device:TPU:0, one launch (start us, length us, event | category | flops | bytes accessed | tf_op | source)
XLA Modules:
  0.0 276.9 jit_solution(872812007503204623)
XLA Ops:
  0.6 0.7 convert_element_type.41
  1.3 0.7 convert_reduce_fusion
  2.1 2.8 %concatenate.6 = f32[3072]{0:T(1024)S(1)} concatenate(f32[1152]{0:T(1024)S(1)} %fusion, bf16[144]{0:T(256)(128)(2,1)} %param.20, bf16[72]{0:T(256)(128)(2,1)} %param.22, bf16[72]{0:T(256)(128)(2,1)} %param.26, f32[96]{0:T(128)S(1)} %broadcast.3, bf16[288]{0:T(512)(128)(2,1)} %param.24, f32[96]{0:T(128)S(1)} %broadcast.3, f32[256]{0:T(256)S(1)} %bitcast.25, f32[896]{0:T(1024)S(1)} %broadcast_in_dim.12), dimensions={0} | concatenate | bytes 23424 | tf_op jit(solution)/shard_map/concatenate | solution.py:1248
  4.8 0.6 reshape.56.small
  5.5 0.8 convert_dynamic-update-slice_fusion
  6.2 0.6 reshape.57.adab
  6.8 254.2 %whole_block.1 = (bf16[256,1152]{1,0:T(8,128)(2,1)}, bf16[256,1152]{1,0:T(8,128)(2,1)}, f32[72,6912]{1,0:T(8,128)}, f32[72,3456]{1,0:T(8,128)}, f32[72,1152]{1,0...) custom-call(bf16[256,1152]{1,0:T(8,128)(2,1)} %bitcast.19, bf16[256,1152]{1,0:T(8,128)(2,1)} %bitcast.20, ...), custom_call_target="tpu_custom_call" | custom-call | tf_op jit(solution)/shard_map/whole_block/pallas_call | solution.py:1270
  261.1 0.0 copy-start.4
  261.1 0.9 fusion.2
  261.9 0.6 dynamic-slice_bitcast_fusion
  262.5 0.8 slice.28
  263.3 0.1 reshape.60
  263.4 0.1 slice.32
  263.5 0.1 slice.30
  263.6 0.7 fusion.1
  264.3 0.8 slice.34
  265.0 0.9 slice.27
  266.0 0.7 dynamic_slice.19
  266.6 0.1 reshape.61
  266.7 0.1 reshape.62
  266.8 0.7 dynamic_slice.23
  267.5 1.9 copy.40
  269.4 0.0 copy-done.4
  269.4 0.8 copy.41
  270.2 1.3 copy.42
  271.5 0.6 copy-done.3
  272.1 0.9 copy.43
  273.1 0.2 copy-done.5
  273.3 0.7 copy.44
  274.0 1.1 copy.45
  275.1 0.7 copy-done.1
  275.8 1.1 copy.46
  (15 shorter events, 0.1 us)
Async XLA Ops:
  261.1 8.3 %copy-start.4 = (bf16[256,1152]{1,0:T(8,128)(2,1)S(1)}, bf16[256,1152]{1,0:T(8,128)(2,1)}, u32[]{:S(2)}) copy-start(bf16[256,1152]{1,0:T(8,128)(2,1)} %get-tuple-element.21) | copy-start | bytes 1769476
  265.0 5.2 %copy-start = (f32[72,6912]{1,0:T(8,128)S(1)}, f32[72,6912]{1,0:T(8,128)}, u32[]{:S(2)}) copy-start(f32[72,6912]{1,0:T(8,128)} %get-tuple-element.48) | copy-start | bytes 5971972
  270.2 1.9 copy-start.3
  272.1 1.2 copy-start.5
  272.1 1.9 copy-start.2
  274.0 1.8 copy-start.1
